TPU v7x, 256 devices: a whole 4x4x8 slice. The times are simulated.
256 devices in a mesh: tok: 64 (over y, z, core), head: 4 (over x).
Axes of the slice: x: 4, y: 4, z: 8, core: 2. Of those that a mesh axis runs over, the one named last changes fastest.
Arguments:
- query_rows: bfloat16 [32768, 4, 1024], P('tok', 'head'), may hold values from -6 to 6
- key_rows: bfloat16 [32768, 4, 128], P('tok', 'head'), may hold values from -6 to 6
- value_rows: bfloat16 [32768, 4, 128], P('tok', 'head'), may hold values from -6 to 6
- output_gradient: bfloat16 [32768, 4, 1024], P('tok', 'head'), may hold values from -6 to 6
- row_logsumexp: bfloat16 [4, 8, 32768], P('head', None, 'tok'), may hold values from 3 to 7
- row_delta_sums: bfloat16 [4, 8, 32768], P('head', None, 'tok'), may hold values from -5 to 5
- segments: int32 [32768], replicated, may hold values from 0 to 32767, as said below
- query_key_value_weight: bfloat16 [4096, 4, 1280], P('tok', 'head'), may hold values from -0.09375 to 0.09375
Outputs:
- grad_input: bfloat16 [32768, 4096], P('tok', 'head')
Inputs may be any that keep to these rules, and one draw needn't show every extreme that they name: `segments`: numbers never fall along the tokens, and every document lies inside one window of 512 consecutive tokens.
All inputs are finite; a program needn't handle non-finite values.
Results may differ from a plain program's by a relative error of at most 0.012.
Values may be sent and summed in bfloat16 or wider, within the bound.
No kernel may reach another device: no remote copies, remote signals or barrier semaphores. Data moves between devices by JAX's collectives and lax.ppermute only.
A program may use at most 128 MiB of HBM per device.

v0:
```python
import jax
import jax.numpy as jnp
import numpy as np
from jax import lax
from jax.sharding import PartitionSpec as P

BLOCK = 128


def pair_lists(block_count):
    query_list = []
    key_list = []
    for query_block in range(block_count):
        for key_block in range(query_block + 1):
            query_list.append(query_block)
            key_list.append(key_block)
    return (np.array(query_list, np.int32), np.array(key_list, np.int32))


def live_pairs(seg_window, query_list, key_list, tile_rows):
    first_seg = jnp.take(seg_window, query_list * tile_rows)
    last_seg = jnp.take(seg_window, key_list * tile_rows + tile_rows - 1)
    return (first_seg == last_seg) | jnp.asarray(query_list == key_list)


def pair_grads(query_tile, dout_tile, key_tile, value_tile, lse_tile, delta_tile, allowed):
    tile_rows, groups, query_width = query_tile.shape
    head_size = key_tile.shape[2]
    heads_per_group = query_width // head_size
    query_heads = query_tile.reshape(tile_rows, groups, heads_per_group, head_size)
    dout_heads = dout_tile.reshape(tile_rows, groups, heads_per_group, head_size)
    scores = jnp.einsum(
        "agrd,bgd->grab", query_heads, key_tile, preferred_element_type=jnp.float32
    ) * head_size ** (-0.5)
    logits = scores - lse_tile.astype(jnp.float32)[:, :, :, None]
    soft_probs = jnp.where(allowed[None, None], jnp.exp(logits), 0.0)
    probs_low = soft_probs.astype(jnp.bfloat16)
    value_gradient = jnp.einsum(
        "grab,agrd->bgd", probs_low, dout_heads, preferred_element_type=jnp.float32
    )
    grad_prob = jnp.einsum(
        "agrd,bgd->grab", dout_heads, value_tile, preferred_element_type=jnp.float32
    )
    grad_score = (soft_probs * (grad_prob - delta_tile.astype(jnp.float32)[:, :, :, None])).astype(
        jnp.bfloat16
    )
    query_gradient = jnp.einsum(
        "grab,bgd->agrd", grad_score, key_tile, preferred_element_type=jnp.float32
    )
    key_gradient = jnp.einsum(
        "grab,agrd->bgd", grad_score, query_heads, preferred_element_type=jnp.float32
    )
    return (query_gradient.reshape(tile_rows, groups, query_width), key_gradient, value_gradient)


def on_device(
    query_rows,
    key_rows,
    value_rows,
    output_gradient,
    row_logsumexp,
    row_delta_sums,
    segments,
    query_key_value_weight,
):
    weight_whole = lax.all_gather(query_key_value_weight, "tok", axis=0, tiled=True)
    window, kv_dev, query_width = query_rows.shape
    head_size = key_rows.shape[2]
    tile_rows = BLOCK
    block_count = window // tile_rows
    query_list, key_list = pair_lists(block_count)
    query_table = jnp.asarray(query_list)
    key_table = jnp.asarray(key_list)
    myself = lax.axis_index("tok")
    own_seg = lax.dynamic_slice_in_dim(segments, myself * window, window)
    own_live = live_pairs(own_seg, query_list, key_list, tile_rows)
    block_ids = jnp.arange(block_count, dtype=jnp.int32)
    query_match = (query_table[:, None] == block_ids[None, :]) & own_live[:, None]
    key_match = key_table[:, None] == block_ids[None, :]
    block_local = jnp.any(query_match[:, :, None] & key_match[:, None, :], axis=0)
    token_local = jnp.repeat(jnp.repeat(block_local, tile_rows, axis=0), tile_rows, axis=1)
    offsets = jnp.arange(window, dtype=jnp.int32)
    allowed_all = (
        (own_seg[:, None] == own_seg[None, :])
        & (offsets[None, :] <= offsets[:, None])
        & token_local
    )
    local_out = pair_grads(
        query_rows,
        output_gradient,
        key_rows,
        value_rows,
        row_logsumexp,
        row_delta_sums,
        allowed_all,
    )
    acc_query = local_out[0].reshape(block_count, tile_rows, kv_dev, query_width)
    acc_key = local_out[1].reshape(block_count, tile_rows, kv_dev, head_size)
    acc_value = local_out[2].reshape(block_count, tile_rows, kv_dev, head_size)
    score_scale = head_size ** (-0.5)
    query_gradient = (acc_query * score_scale).reshape(window, kv_dev, query_width)
    key_gradient = (acc_key * score_scale).reshape(window, kv_dev, head_size)
    value_gradient = acc_value.reshape(window, kv_dev, head_size)
    stacked_gradients = (
        jnp.concatenate([query_gradient, key_gradient, value_gradient], axis=2)
        .astype(jnp.bfloat16)
        .reshape(window, -1)
    )
    flat_piece = weight_whole.reshape(weight_whole.shape[0], -1)
    partial_sum = lax.dot_general(
        stacked_gradients, flat_piece, (((1,), (1,)), ((), ())), preferred_element_type=jnp.float32
    )
    summed = lax.psum_scatter(
        partial_sum.astype(jnp.bfloat16), "head", scatter_dimension=1, tiled=True
    )
    return summed


def solution(mesh):
    placed = (
        P("tok", "head", None),
        P("tok", "head", None),
        P("tok", "head", None),
        P("tok", "head", None),
        P("head", None, "tok"),
        P("head", None, "tok"),
        P(),
        P("tok", "head", None),
    )
    return jax.shard_map(
        on_device, mesh=mesh, in_specs=placed, out_specs=P("tok", "head"), check_vma=False
    )
```

profile of v0, /device:TPU:1, one launch (start us, length us, event | category | flops | bytes accessed | tf_op | source)
XLA Modules:
  0.0 165.1 jit_solution(10995759829409910202)
XLA Ops:
  6.5 0.0 copy-start
  6.5 0.0 copy-start.1
  6.5 0.0 all-gather.2.cloned.1.call-start
  6.5 0.7 all-gather.2.cloned.1.call-update
  7.3 0.0 reduce-scatter.2.cloned.1.call-start
  7.3 0.8 dynamic_slice.3
  8.1 0.7 pad_clamp_fusion.1
  8.7 0.7 gather_fusion
  9.4 0.7 pad_clamp_fusion
  10.1 0.7 gather_fusion.1
  10.7 0.7 compare_or_fusion
  11.4 0.7 iota_compare_fusion.1
  12.1 0.2 and_reduce_fusion
  12.2 0.1 copy.22
  12.3 0.1 broadcast_bitcast_fusion
  12.4 0.2 fusion.29
  12.7 1.5 copy.36
  14.2 1.5 copy.37
  15.7 0.7 bitcast_convert_fusion.1
  16.4 0.7 bitcast_convert_fusion
  17.1 0.0 copy-done
  17.1 1.2 fusion.32
  18.3 0.0 copy-done.1
  18.3 2.8 %fusion.11 = bf16[8,512,512]{1,2,0:T(8,128)(2,1)S(1)} fusion(f32[512,512,8]{1,0,2:T(8,128)S(1)} %fusion.32, f32[8,512]{1,0:T(8,128)S(1)} %bitcast_convert_fusion, f32[8,512]{1,0:T(8,128)S(1)} %bitcast_convert_fusion.1, pred[512,512]{0,1:T(8,128)(4,1)S(1)} %fusion.29, bf16[512,8,128]{0,2,1:T(8,128)(2,1)S(1)} %bitcast.99, bf16[512,1,128]{2,0,1:T(8,128)(2,1)S(1)} %copy-done.1), kind=kOutput, calls=%fused_computation.13 | convolution fusion | flops 549453824 | bytes 14057472 | tf_op jit(solution)/shard_map/agrd,bgd->grab/dot_general | solution.py:41
  21.2 0.8 multiply_convert_fusion
  22.0 2.1 %fusion.27 = bf16[512,128]{0,1:T(8,128)(2,1)} fusion(bf16[8,512,512]{1,2,0:T(8,128)(2,1)S(1)} %fusion.11, bf16[512,8,128]{0,2,1:T(8,128)(2,1)S(1)} %bitcast.98), kind=kOutput, calls=%fused_computation.26 | convolution fusion | flops 537001984 | bytes 5373952 | tf_op jit(solution)/shard_map/grab,agrd->bgd/dot_general | solution.py:50
  24.1 0.0 copy-start.2
  24.1 1.9 %fusion.24 = bf16[512,128]{0,1:T(8,128)(2,1)S(1)} fusion(bf16[512,8,128]{0,2,1:T(8,128)(2,1)S(1)} %bitcast.100, f32[512,512,8]{1,0,2:T(8,128)S(1)} %fusion.32, f32[8,512]{1,0:T(8,128)S(1)} %bitcast_convert_fusion.1, pred[512,512]{0,1:T(8,128)(4,1)S(1)} %fusion.29), kind=kOutput, calls=%fused_computation.25 | convolution fusion | flops 545325056 | bytes 9846784 | tf_op jit(solution)/shard_map/grab,agrd->bgd/dot_general | solution.py:38
  26.0 74.8 %all-gather.2.cloned.1.call-done = bf16[4096,1,1280]{2,0,1:T(8,128)(2,1)} async-done(((bf16[64,1,1280]{2,0,1:T(8,128)(2,1)}), bf16[4096,1,1280]{2,0,1:T(8,128)(2,1)}) %all-gather.2.cloned.1.call-update) | async-done | bytes 10485776 | tf_op jit(solution)/shard_map/all_gather | solution.py:66
  100.8 0.0 copy-done.2
  100.8 11.2 %fusion.7 = bf16[512,4096]{1,0:T(8,128)(2,1)} fusion(bf16[4096,1,1280]{2,0,1:T(8,128)(2,1)} %all-gather.2.cloned.1.call-done, bf16[512,128]{0,1:T(8,128)(2,1)S(1)} %fusion.24, bf16[512,128]{0,1:T(8,128)(2,1)S(1)} %copy-done.2, bf16[512,1024]{0,1:T(8,128)(2,1)S(1)} %bitcast.101), kind=kOutput, calls=%fused_computation.11 | convolution fusion | flops 5374738432 | bytes 15990784 | tf_op jit(solution)/shard_map/dot_general | solution.py:110
  112.0 0.0 reduce-scatter.2.cloned.1.call-update
  112.1 46.1 %reduce-scatter.2.cloned.1.call-done = bf16[512,1024]{1,0:T(8,128)(2,1)} async-done(((bf16[512,4096]{1,0:T(8,128)(2,1)}), bf16[512,1024]{1,0:T(8,128)(2,1)}) %reduce-scatter.2.cloned.1.call-update) | async-done | bytes 1048592 | tf_op jit(solution)/shard_map/reduce_scatter | solution.py:113
  (1 shorter events, 0.0 us)
Async XLA Ops:
  6.5 10.5 %copy-start = (bf16[512,1,128]{2,0,1:T(8,128)(2,1)S(1)}, bf16[512,1,128]{2,0,1:T(8,128)(2,1)}, u32[]{:S(2)}) copy-start(bf16[512,1,128]{2,0,1:T(8,128)(2,1)} %param.16) | copy-start | bytes 393220
  6.5 11.8 %copy-start.1 = (bf16[512,1,128]{2,0,1:T(8,128)(2,1)S(1)}, bf16[512,1,128]{2,0,1:T(8,128)(2,1)}, u32[]{:S(2)}) copy-start(bf16[512,1,128]{2,0,1:T(8,128)(2,1)} %param.17) | copy-start | bytes 393220
  6.5 94.3 %all-gather.2.cloned.1.call-start = ((), (), s32[]{:S(2)}) async-start(), calls=%async_computation.1 | async-start | bytes 10649600 | tf_op jit(solution)/shard_map/all_gather | solution.py:66
  7.3 151.0 %reduce-scatter.2.cloned.1.call-start = ((), (), s32[]{:S(2)}) async-start(), calls=%async_computation.2 | async-start | bytes 5242880 | tf_op jit(solution)/shard_map/reduce_scatter | solution.py:113
  24.1 76.7 %copy-start.2 = (bf16[512,128]{0,1:T(8,128)(2,1)S(1)}, bf16[512,128]{0,1:T(8,128)(2,1)}, u32[]{:S(2)}) copy-start(bf16[512,128]{0,1:T(8,128)(2,1)} %fusion.27) | copy-start | bytes 393220
Sparse Core Ops, SparseCore 0:
  10.1 90.6 all-gather.1
  112.2 45.9 reduce-scatter.1
where the time goes:
time: 165 us
  waiting for transfers between devices  122 us (74%)
  matrix products  20.1 us (12%)
  between operations  13.5 us (8%)
  local copies, waits for them, and re-layouts  5.3 us (3%)
  other arithmetic  4.45 us (3%)
    all_gather x1, waiting for transfers between devices, on_device(): lax.all_gather(query_key_value_weight, 'tok', axis=0, tiled=True)  74.8 us
    reduce_scatter x1, waiting for transfers between devices, on_device(): lax.psum_scatter(partial_sum.astype(jnp.bfloat16), 'head', scatter_dimens...  46.1 us
    dot_general x1, matrix products, on_device(): lax.dot_general(stacked_gradients, flat_piece, (((1,), (1,)), ((), ())),...  11.2 us
  transfers between devices with their start and end apart: 2, of which 2 were waited for; matrix products, arithmetic and copies ran while one was open for 11% of the time, Pallas kernels for 0%

commit v1 on v0

--- a/solution.py
+++ b/solution.py
@@ -63,7 +63,10 @@
     segments,
     query_key_value_weight,
 ):
-    weight_whole = lax.all_gather(query_key_value_weight, "tok", axis=0, tiled=True)
+    weight_whole = jnp.concatenate(
+        lax.all_to_all(jnp.stack([query_key_value_weight] * lax.axis_size("tok")), "tok", 0, 0),
+        axis=0,
+    )
     window, kv_dev, query_width = query_rows.shape
     head_size = key_rows.shape[2]
     tile_rows = BLOCK

time: 165 us -> 321 us (1.95)
  waiting for transfers between devices: 122 us -> 264 us
  starting transfers between devices: 0.04 us -> 13.5 us
  local copies, waits for them, and re-layouts: 5.3 us -> 9.48 us
  other arithmetic: 4.45 us -> 0.42 us
    all_to_all x0 -> x1, waiting for transfers between devices: none -> 218 us  [on_device(): lax.all_to_all(jnp.stack([query_key_value_weight] * lax.axis_size('tok'))...]
    all_gather x1 -> x0, waiting for transfers between devices: 74.8 us -> none  [on_device(): lax.all_gather(query_key_value_weight, 'tok', axis=0, tiled=True)]
    all_to_all x0 -> x1, starting transfers between devices: none -> 13.5 us  [on_device(): lax.all_to_all(jnp.stack([query_key_value_weight] * lax.axis_size('tok'))...]
    another operation x2 -> x3, local copies, waits for them, and re-layouts: 3 us -> 7.12 us  [the longest x1 6.04 us: on_device(): jnp.stack([query_key_value_weight] * lax.axis_size('tok'))]
  transfers between devices with their start and end apart: 2 -> 2, of which waited for: 2 -> 2; matrix products, arithmetic and copies ran while one was open for 11% -> 4% of each run, Pallas kernels for 0% -> 0%
where the time goes in v1:
time: 321 us
  waiting for transfers between devices  264 us (82%)
  matrix products  20 us (6%)
  between operations  13.6 us (4%)
  starting transfers between devices  13.5 us (4%)
  local copies, waits for them, and re-layouts  9.48 us (3%)
    all_to_all x1, waiting for transfers between devices, on_device(): lax.all_to_all(jnp.stack([query_key_value_weight] * lax.axis_size('tok'))...  218 us
    reduce_scatter x1, waiting for transfers between devices, on_device(): lax.psum_scatter(partial_sum.astype(jnp.bfloat16), 'head', scatter_dimens...  46.3 us
    all_to_all x1, starting transfers between devices, on_device(): lax.all_to_all(jnp.stack([query_key_value_weight] * lax.axis_size('tok'))...  13.5 us
    dot_general x1, matrix products, on_device(): lax.dot_general(stacked_gradients, flat_piece, (((1,), (1,)), ((), ())),...  11.2 us
  transfers between devices with their start and end apart: 2, of which 2 were waited for; matrix products, arithmetic and copies ran while one was open for 4% of the time, Pallas kernels for 0%

profile of v1, /device:TPU:1, one launch (start us, length us, event | category | flops | bytes accessed | tf_op | source)
XLA Modules:
  0.0 321.2 jit_solution(1353972575943222868)
XLA Ops:
  6.5 0.0 copy-start
  6.5 6.0 %stack.2 = bf16[64,64,1,1280]{3,1,2,0:T(8,128)(2,1)} broadcast(bf16[64,1280]{1,0:T(8,128)(2,1)} %bitcast.100), dimensions={1,3} | broadcast | bytes 10649600 | tf_op jit(solution)/shard_map/stack | solution.py:67
  12.6 0.0 copy-start.8
  12.6 0.0 copy-start.7
  12.6 0.0 copy-start.9
  12.6 0.0 copy-start.5
  12.6 0.0 copy-start.6
  12.6 0.0 copy-start.1
  12.6 0.0 copy-start.2
  12.6 0.0 copy-start.3
  12.6 0.0 copy-start.4
  12.6 13.5 %all-to-all-start = ((bf16[64,64,1,1280]{3,1,2,0:T(8,128)(2,1)}), bf16[64,64,1,1280]{3,1,2,0:T(8,128)(2,1)}, u32[]{:S(2)}, u32[]{:S(2)}) async-start(bf16[64,64,1,1280]{3,1,2,0:T(8,128)(2,1)} %stack.2), calls=%async_computation | async-start | bytes 20971520 | tf_op jit(solution)/shard_map/all_to_all | solution.py:67
  26.1 0.0 reduce-scatter.2.cloned.1.call-start
  26.2 0.8 dynamic_slice.3
  26.9 0.0 copy-done.8
  26.9 0.7 gather_fusion
  27.6 0.0 copy-done.7
  27.6 0.7 gather_fusion.1
  28.3 0.0 copy-done.9
  28.3 0.0 copy-done.5
  28.3 0.0 copy-done.6
  28.3 0.2 and_reduce_fusion
  28.5 0.1 copy.30
  28.6 0.1 broadcast_bitcast_fusion
  28.7 0.2 fusion.24
  28.9 0.0 copy-done.1
  28.9 0.5 copy.44
  29.5 0.0 copy-done.2
  29.5 0.5 copy.45
  30.1 0.0 copy-done.3
  30.1 0.0 copy-start.10
  30.1 0.0 copy-done.4
  30.1 0.0 copy-done
  30.1 1.2 fusion.27
  31.4 0.0 copy-done.10
  31.4 2.8 fusion.6
  34.2 0.8 multiply_convert_fusion
  35.0 2.1 fusion.22
  37.1 0.0 copy-start.11
  37.1 1.9 fusion.19
  39.0 217.8 %all-to-all-done = bf16[64,64,1,1280]{3,1,2,0:T(8,128)(2,1)} async-done(((bf16[64,64,1,1280]{3,1,2,0:T(8,128)(2,1)}), bf16[64,64,1,1280]{3,1,2,0:T(8,128)(2,1)}, u32[]{:S(2)}, u32[]{:S(2)}) %all-to-all-start) | async-done | bytes 10485792 | tf_op jit(solution)/shard_map/all_to_all | solution.py:67
  256.9 0.0 copy-done.11
  256.9 11.2 %convolution_convert_fusion = bf16[512,4096]{1,0:T(8,128)(2,1)} fusion(bf16[4096,1280]{1,0:T(8,128)(2,1)} %bitcast.21, bf16[512,128]{0,1:T(8,128)(2,1)S(1)} %fusion.19, bf16[512,128]{0,1:T(8,128)(2,1)S(1)} %copy-done.11, bf16[512,1024]{0,1:T(8,128)(2,1)S(1)} %bitcast.99), kind=kOutput, calls=%fused_computation.9 | convolution fusion | flops 5374738432 | bytes 15990784 | tf_op jit(solution)/shard_map/dot_general | solution.py:113
  268.1 0.0 reduce-scatter.2.cloned.1.call-update
  268.1 46.3 %reduce-scatter.2.cloned.1.call-done = bf16[512,1024]{1,0:T(8,128)(2,1)} async-done(((bf16[512,4096]{1,0:T(8,128)(2,1)}), bf16[512,1024]{1,0:T(8,128)(2,1)}) %reduce-scatter.2.cloned.1.call-update) | async-done | bytes 1048592 | tf_op jit(solution)/shard_map/reduce_scatter | solution.py:116
  (7 shorter events, 0.0 us)
Async XLA Ops:
  6.5 23.6 %copy-start = (bf16[512,1,128]{2,0,1:T(8,128)(2,1)S(1)}, bf16[512,1,128]{2,0,1:T(8,128)(2,1)}, u32[]{:S(2)}) copy-start(bf16[512,1,128]{2,0,1:T(8,128)(2,1)} %param.16) | copy-start | bytes 393220
  12.6 14.4 %copy-start.8 = (s32[10]{0:T(128)S(1)}, s32[10]{0:T(128)}, u32[]{:S(2)}) copy-start(s32[10]{0:T(128)} %constant.70) | copy-start | bytes 124
  12.6 15.0 %copy-start.7 = (s32[10]{0:T(128)S(1)}, s32[10]{0:T(128)}, u32[]{:S(2)}) copy-start(s32[10]{0:T(128)} %constant.71) | copy-start | bytes 124
  12.6 15.7 %copy-start.9 = (pred[10]{0:T(512)(128)(4,1)S(1)}, pred[10]{0:T(512)(128)(4,1)}, u32[]{:S(2)}) copy-start(pred[10]{0:T(512)(128)(4,1)} %constant.44.clone) | copy-start | bytes 34
  12.6 15.7 %copy-start.5 = (s32[10]{0:T(128)S(1)}, s32[10]{0:T(128)}, u32[]{:S(2)}) copy-start(s32[10]{0:T(128)} %constant.20.clone) | copy-start | bytes 124
  12.6 15.7 %copy-start.6 = (s32[10]{0:T(128)S(1)}, s32[10]{0:T(128)}, u32[]{:S(2)}) copy-start(s32[10]{0:T(128)} %constant.19.clone) | copy-start | bytes 124
  12.6 16.3 %copy-start.1 = (bf16[512,1,1024]{2,0,1:T(8,128)(2,1)S(1)}, bf16[512,1,1024]{2,0,1:T(8,128)(2,1)}, u32[]{:S(2)}) copy-start(bf16[512,1,1024]{2,0,1:T(8,128)(2,1)} %param.15) | copy-start | bytes 3145732
  12.6 16.9 %copy-start.2 = (bf16[512,1,1024]{2,0,1:T(8,128)(2,1)S(1)}, bf16[512,1,1024]{2,0,1:T(8,128)(2,1)}, u32[]{:S(2)}) copy-start(bf16[512,1,1024]{2,0,1:T(8,128)(2,1)} %param.18) | copy-start | bytes 3145732
  12.6 17.4 %copy-start.3 = (bf16[1,8,512]{2,1,0:T(8,128)(2,1)S(1)}, bf16[1,8,512]{2,1,0:T(8,128)(2,1)}, u32[]{:S(2)}) copy-start(bf16[1,8,512]{2,1,0:T(8,128)(2,1)} %param.19) | copy-start | bytes 24580
  12.6 17.5 %copy-start.4 = (bf16[1,8,512]{2,1,0:T(8,128)(2,1)S(1)}, bf16[1,8,512]{2,1,0:T(8,128)(2,1)}, u32[]{:S(2)}) copy-start(bf16[1,8,512]{2,1,0:T(8,128)(2,1)} %param.20) | copy-start | bytes 24580
  12.6 244.2 %all-to-all-start = ((bf16[64,64,1,1280]{3,1,2,0:T(8,128)(2,1)}), bf16[64,64,1,1280]{3,1,2,0:T(8,128)(2,1)}, u32[]{:S(2)}, u32[]{:S(2)}) async-start(bf16[64,64,1,1280]{3,1,2,0:T(8,128)(2,1)} %stack.2), calls=%async_computation | async-start | bytes 20971520 | tf_op jit(solution)/shard_map/all_to_all | solution.py:67
  26.1 288.2 %reduce-scatter.2.cloned.1.call-start = ((), (), s32[]{:S(2)}) async-start(), calls=%async_computation.2 | async-start | bytes 5242880 | tf_op jit(solution)/shard_map/reduce_scatter | solution.py:116
  30.1 1.3 copy-start.10
  37.1 219.8 %copy-start.11 = (bf16[512,128]{0,1:T(8,128)(2,1)S(1)}, bf16[512,128]{0,1:T(8,128)(2,1)}, u32[]{:S(2)}) copy-start(bf16[512,128]{0,1:T(8,128)(2,1)} %fusion.22) | copy-start | bytes 393220
Sparse Core Ops, SparseCore 0:
  268.2 46.1 reduce-scatter.1
